TPU v7x, 32 devices: a whole 2x2x4 slice. The times are simulated.
32 devices in a mesh: batch: 4 (over z), seq: 2 (over core), ch: 4 (over y, x).
Axes of the slice: x: 2, y: 2, z: 4, core: 2. Of those that a mesh axis runs over, the one named last changes fastest.
Arguments:
- inputs: bfloat16 [16, 1280, 2048], P('batch', 'ch', 'seq'), may hold values from -6 to 6
- segment_ids: int32 [16, 2048], P('batch', 'seq'), may hold values from 0 to 7, never falling along the last dimension, each value on 1 to 512 neighbouring positions
- norm0_gain: float32 [1280], P('ch'), may hold values from 0.1 to 1.9
- norm0_shift: float32 [1280], P('ch'), may hold values from -3 to 3
- w_inner: bfloat16 [1280, 640], P('ch'), may hold values from -0.15625 to 0.15625
- b_inner: float32 [640], P('ch'), may hold values from -3 to 3
- norm1_gain: float32 [640], P('ch'), may hold values from 0.1 to 1.9
- norm1_shift: float32 [640], P('ch'), may hold values from -3 to 3
- w_conv: bfloat16 [5, 640, 640], P(None, 'ch'), may hold values from -0.109375 to 0.109375
- b_conv: float32 [640], P('ch'), may hold values from -3 to 3
- norm2_gain: float32 [640], P('ch'), may hold values from 0.1 to 1.9
- norm2_shift: float32 [640], P('ch'), may hold values from -3 to 3
- w_outer: bfloat16 [640, 1280], P('ch'), may hold values from -0.25 to 0.25
- b_outer: float32 [1280], P('ch'), may hold values from -3 to 3
- cotangent: bfloat16 [16, 1280, 2048], P('batch', 'ch', 'seq'), may hold values from -6 to 6
Outputs:
- output: bfloat16 [16, 1280, 2048], P('batch', 'ch', 'seq')
- input_grad: bfloat16 [16, 1280, 2048], P('batch', 'ch', 'seq')
- grad_norm0_gain: float32 [1280], P('ch')
- grad_norm0_shift: float32 [1280], P('ch')
- grad_w_inner: float32 [1280, 640], P('ch')
- grad_b_inner: float32 [640], P('ch')
- grad_norm1_gain: float32 [640], P('ch')
- grad_norm1_shift: float32 [640], P('ch')
- grad_w_conv: float32 [5, 640, 640], P(None, 'ch')
- grad_b_conv: float32 [640], P('ch')
- grad_norm2_gain: float32 [640], P('ch')
- grad_norm2_shift: float32 [640], P('ch')
- grad_w_outer: float32 [640, 1280], P('ch')
- grad_b_outer: float32 [1280], P('ch')
Inputs may be any that keep to these rules, and one draw needn't show every extreme that they name: `segment_ids`: along a row the ids never fall; each protein is one run of 1 to 512 residues, one run of each row has exactly 512, and every row holds all 8 ids.
All inputs are finite; a program needn't handle non-finite values.
Results may differ from a plain program's by a relative error of at most 0.0065.
Values may be sent and summed in bfloat16 or wider, within the bound.
A program may use at most 192 MiB of HBM per device.

v0:
```python
import jax
import jax.numpy as jnp
from jax import lax
from jax.sharding import PartitionSpec as P

KERNEL_TAPS = 5
DILATION_SPACING = 32


EPSILON = 1e-05


def extended(x, sides, width):
    for axis, dim in sides:
        size, length = (lax.axis_size(axis), x.shape[dim])
        up = [(i, (i + 1) % size) for i in range(size - 1)]
        down = [(j, i) for i, j in up]
        last = lax.slice_in_dim(x, length - width, length, axis=dim)
        leading = lax.slice_in_dim(x, 0, width, axis=dim)
        before = lax.ppermute(last, axis, up)
        after = lax.ppermute(leading, axis, down)
        x = jnp.concatenate([before, x, after], axis=dim)
    return x


def gelu_exact(values):
    return jax.nn.gelu(values, approximate=False)


def gelu_back(point, grad):
    return jax.vjp(gelu_exact, point)[1](grad)[0]


def channel_sums(first, second):
    return lax.psum((first, second), "ch")


def normalize(values, gain, shift):
    width = values.shape[1] * lax.axis_size("ch")
    total, squares = channel_sums(
        jnp.sum(values, axis=1, keepdims=True), jnp.sum(values * values, axis=1, keepdims=True)
    )
    center = total / width
    spread = squares / width - center * center
    scale = lax.rsqrt(spread + EPSILON)
    unit = (values - center) * scale
    return (unit * gain[:, None] + shift[:, None], unit, scale)


def normalize_back(grad, unit, scale, gain):
    width = grad.shape[1] * lax.axis_size("ch")
    scaled = grad * gain[:, None]
    first, second = channel_sums(
        jnp.sum(scaled, axis=1, keepdims=True), jnp.sum(scaled * unit, axis=1, keepdims=True)
    )
    return scale * (scaled - first / width - unit * (second / width))


def shifted_taps(wide, wide_ids, own_ids, tap_displacements, border_extent):
    length = own_ids.shape[1]
    pieces = []
    for tap_displacement in tap_displacements:
        lower = border_extent + tap_displacement
        shifted = wide[:, :, lower : lower + length]
        matching = wide_ids[:, lower : lower + length] == own_ids
        pieces.append(jnp.where(matching[:, None, :], shifted, jnp.zeros_like(shifted)))
    return jnp.stack(pieces, axis=1)


def local(
    inputs,
    segment_ids,
    norm0_gain,
    norm0_shift,
    w_inner,
    b_inner,
    norm1_gain,
    norm1_shift,
    w_conv,
    b_conv,
    norm2_gain,
    norm2_shift,
    w_outer,
    b_outer,
    cotangent,
):
    border_extent = 2 * DILATION_SPACING
    tap_displacements = [
        (tap_stride - KERNEL_TAPS // 2) * DILATION_SPACING for tap_stride in range(KERNEL_TAPS)
    ]
    back_offsets = [-tap_displacement for tap_displacement in tap_displacements]
    residual = inputs.astype(jnp.float32)
    normed0, unit0, scale0 = normalize(residual, norm0_gain, norm0_shift)
    hidden0 = gelu_exact(normed0).astype(jnp.bfloat16)
    inner_terms = jnp.einsum("sdl,dh->shl", hidden0, w_inner, preferred_element_type=jnp.float32)
    inner = lax.psum_scatter(inner_terms, "ch", scatter_dimension=1, tiled=True) + b_inner[:, None]
    normed1, unit1, scale1 = normalize(inner, norm1_gain, norm1_shift)
    hidden1 = gelu_exact(normed1).astype(jnp.bfloat16)
    own_ids = segment_ids + 1
    wide_ids = extended(own_ids, (("seq", 1),), border_extent)
    wide_hidden = extended(hidden1, (("seq", 2),), border_extent)
    taps = shifted_taps(wide_hidden, wide_ids, own_ids, tap_displacements, border_extent)
    seqs, width, length = hidden1.shape
    taps_flat = taps.reshape(seqs, KERNEL_TAPS * width, length)
    kernel_flat = w_conv.reshape(KERNEL_TAPS * width, w_conv.shape[2])
    conv_terms = jnp.einsum(
        "scl,ch->shl", taps_flat, kernel_flat, preferred_element_type=jnp.float32
    )
    mixed = lax.psum_scatter(conv_terms, "ch", scatter_dimension=1, tiled=True) + b_conv[:, None]
    normed2, unit2, scale2 = normalize(mixed, norm2_gain, norm2_shift)
    hidden2 = gelu_exact(normed2).astype(jnp.bfloat16)
    outer_terms = jnp.einsum("shl,hd->sdl", hidden2, w_outer, preferred_element_type=jnp.float32)
    branch = lax.psum_scatter(outer_terms, "ch", scatter_dimension=1, tiled=True)
    output = (residual + branch + b_outer[:, None]).astype(jnp.bfloat16)
    piece = lax.all_gather(cotangent, "ch", axis=1, tiled=True)
    block = w_outer
    hidden_gradient = jnp.einsum("snl,hn->shl", piece, block, preferred_element_type=jnp.float32)
    part = jnp.einsum("shl,snl->hn", hidden2, piece, preferred_element_type=jnp.float32)
    grad_weight = part
    grad_hidden2 = hidden_gradient
    grad_w_outer = grad_weight
    grad_b_outer = jnp.sum(cotangent.astype(jnp.float32), axis=(0, 2))
    grad_normed2 = gelu_back(normed2, grad_hidden2)
    grad_norm2_gain = jnp.sum(grad_normed2 * unit2, axis=(0, 2))
    grad_norm2_shift = jnp.sum(grad_normed2, axis=(0, 2))
    grad_mixed = normalize_back(grad_normed2, unit2, scale2, norm2_gain).astype(jnp.bfloat16)
    grad_b_conv = jnp.sum(grad_mixed.astype(jnp.float32), axis=(0, 2))
    wide_grad = extended(grad_mixed, (("seq", 2),), border_extent)
    piece = lax.all_gather(wide_grad, "ch", axis=1, tiled=True)
    count = piece.shape[1]
    back_taps = shifted_taps(piece, wide_ids, own_ids, back_offsets, border_extent)
    back_flat = back_taps.reshape(seqs, KERNEL_TAPS * count, length)
    kernel_back = jnp.transpose(w_conv, (0, 2, 1)).reshape(KERNEL_TAPS * count, width)
    hidden_gradient = jnp.einsum(
        "sml,mc->scl", back_flat, kernel_back, preferred_element_type=jnp.float32
    )
    center = piece[:, :, border_extent : border_extent + length]
    part = jnp.einsum("sml,snl->mn", taps_flat, center, preferred_element_type=jnp.float32).reshape(
        KERNEL_TAPS, width, count
    )
    grad_kernel = part
    grad_hidden1 = hidden_gradient
    grad_normed1 = gelu_back(normed1, grad_hidden1)
    grad_norm1_gain = jnp.sum(grad_normed1 * unit1, axis=(0, 2))
    grad_norm1_shift = jnp.sum(grad_normed1, axis=(0, 2))
    grad_inner = normalize_back(grad_normed1, unit1, scale1, norm1_gain).astype(jnp.bfloat16)
    grad_b_inner = jnp.sum(grad_inner.astype(jnp.float32), axis=(0, 2))
    piece = lax.all_gather(grad_inner, "ch", axis=1, tiled=True)
    block = w_inner
    hidden_gradient = jnp.einsum("snl,dn->sdl", piece, block, preferred_element_type=jnp.float32)
    part = jnp.einsum("sdl,snl->dn", hidden0, piece, preferred_element_type=jnp.float32)
    grad_weight = part
    grad_normed0 = gelu_back(normed0, hidden_gradient)
    grad_norm0_gain = jnp.sum(grad_normed0 * unit0, axis=(0, 2))
    grad_norm0_shift = jnp.sum(grad_normed0, axis=(0, 2))
    input_grad = (
        cotangent.astype(jnp.float32) + normalize_back(grad_normed0, unit0, scale0, norm0_gain)
    ).astype(jnp.bfloat16)
    totals = lax.psum(
        (
            grad_norm0_gain,
            grad_norm0_shift,
            grad_weight,
            grad_b_inner,
            grad_norm1_gain,
            grad_norm1_shift,
            grad_kernel,
            grad_b_conv,
            grad_norm2_gain,
            grad_norm2_shift,
            grad_w_outer,
            grad_b_outer,
        ),
        ("batch", "seq"),
    )
    return (
        output,
        input_grad,
        totals[0],
        totals[1],
        totals[2],
        totals[3],
        totals[4],
        totals[5],
        totals[6],
        totals[7],
        totals[8],
        totals[9],
        totals[10],
        totals[11],
    )


def solution(mesh):
    return jax.shard_map(
        local,
        mesh=mesh,
        in_specs=(
            P("batch", "ch", "seq"),
            P("batch", "seq"),
            P("ch"),
            P("ch"),
            P("ch", None),
            P("ch"),
            P("ch"),
            P("ch"),
            P(None, "ch", None),
            P("ch"),
            P("ch"),
            P("ch"),
            P("ch", None),
            P("ch"),
            P("batch", "ch", "seq"),
        ),
        out_specs=(
            P("batch", "ch", "seq"),
            P("batch", "ch", "seq"),
            P("ch"),
            P("ch"),
            P("ch", None),
            P("ch"),
            P("ch"),
            P("ch"),
            P(None, "ch", None),
            P("ch"),
            P("ch"),
            P("ch"),
            P("ch", None),
            P("ch"),
        ),
        check_vma=False,
    )
```

profile of v0, /device:TPU:0, one launch (start us, length us, event | category | flops | bytes accessed | tf_op | source)
XLA Modules:
  0.0 1400.8 jit_solution(3146654529673238040)
XLA Ops:
  7.3 2.6 convert_reduce_fusion
  9.8 17.8 %all-reduce.10 = (f32[4,1,1024]{2,0,1:T(4,128)S(1)}, f32[4,1,1024]{2,0,1:T(4,128)S(1)}) all-reduce(f32[4,1,1024]{2,0,1:T(4,128)S(1)} %bitcast.197, f32[4,1,1024]{2,0,1:T(4,128)S(1)} %bitcast.196), channel_id=1, replica_groups=mesh['batch'=4,'seq'=2,'ch'=4] {'ch'}, use_global_device_ids=true, to_apply=%region_3.0 | all-reduce | flops 8192 | bytes 65536 | tf_op jit(solution)/shard_map/psum | solution.py:35
  27.7 14.6 %multiply_convert_fusion = (bf16[4,320,1024]{2,1,0:T(8,128)(2,1)S(1)}, f32[4,320,1024]{2,1,0:T(8,128)}) fusion(bf16[4,320,1024]{2,1,0:T(8,128)(2,1)} %param.15, f32[320]{0:T(512)S(1)} %copy-done.34, f32[320]{0:T(512)S(1)} %copy-done.28, f32[4,1024]{1,0:T(4,128)S(1)} %get-tuple-element.117, f32[4,1024]{1,0:T(4,128)S(1)} %get-tuple-element.116), kind=kLoop, calls=%fused_computation.51 | loop fusion | flops 91750400 | bytes 10521088 | tf_op jit(solution)/shard_map/convert_element_type | solution.py:94
  43.8 5.7 convolution_bitcast_fusion.1
  49.6 12.9 copy.63
  64.5 3.0 collective-permute-start
  68.8 199.4 %all-reduce.16.cloned.1.call-done = f32[4,640,1024]{2,0,1:T(4,128)} async-done(((f32[4,640,1024]{2,0,1:T(4,128)}), f32[4,640,1024]{2,0,1:T(4,128)}) %all-reduce.16.cloned.1.call-update) | async-done | bytes 10485776
  268.3 2.3 constant_dynamic-slice_fusion.2
  273.6 15.7 %all-reduce.9 = (f32[4,1,1024]{2,0,1:T(4,128)S(1)}, f32[4,1,1024]{2,0,1:T(4,128)S(1)}) all-reduce(f32[4,1,1024]{2,0,1:T(4,128)S(1)} %bitcast.193, f32[4,1,1024]{2,0,1:T(4,128)S(1)} %bitcast.192), channel_id=1, replica_groups=mesh['batch'=4,'seq'=2,'ch'=4] {'ch'}, use_global_device_ids=true, to_apply=%region_8.0 | all-reduce | flops 8192 | bytes 65536 | tf_op jit(solution)/shard_map/psum | solution.py:35
  289.3 8.2 multiply_convert_fusion.4
  302.3 7.1 bitcast_dynamic-update-slice_fusion.1
  311.1 2.7 copy-done.17
  313.8 9.1 convolution_bitcast_fusion.2
  322.9 12.9 copy.65
  336.6 206.1 %all-reduce.18.cloned.1.call-done = f32[4,640,1024]{2,0,1:T(4,128)} async-done(((f32[4,640,1024]{2,0,1:T(4,128)}), f32[4,640,1024]{2,0,1:T(4,128)}) %all-reduce.18.cloned.1.call-update) | async-done | bytes 10485776
  547.9 16.7 %all-reduce.8 = (f32[4,1,1024]{2,0,1:T(4,128)S(1)}, f32[4,1,1024]{2,0,1:T(4,128)S(1)}) all-reduce(f32[4,1,1024]{2,0,1:T(4,128)S(1)} %bitcast.195, f32[4,1,1024]{2,0,1:T(4,128)S(1)} %bitcast.194), channel_id=1, replica_groups=mesh['batch'=4,'seq'=2,'ch'=4] {'ch'}, use_global_device_ids=true, to_apply=%region_13.14 | all-reduce | flops 8192 | bytes 65536 | tf_op jit(solution)/shard_map/psum | solution.py:35
  564.7 9.1 multiply_convert_fusion.3
  573.8 76.4 %all-gather.4.cloned.1.call-done = bf16[4,1280,1024]{2,1,0:T(8,128)(2,1)} async-done(((bf16[4,320,1024]{2,1,0:T(8,128)(2,1)}), bf16[4,1280,1024]{2,1,0:T(8,128)(2,1)}) %all-gather.4.cloned.1.call-update) | async-done | bytes 10485776 | tf_op jit(solution)/shard_map/all_gather | solution.py:115
  650.2 12.3 multiply_reduce_fusion.1
  662.5 15.3 %all-reduce.7 = (f32[4,1,1024]{2,0,1:T(4,128)S(1)}, f32[4,1,1024]{2,0,1:T(4,128)S(1)}) all-reduce(f32[4,1,1024]{2,0,1:T(4,128)S(1)} %bitcast.200, f32[4,1,1024]{2,0,1:T(4,128)S(1)} %bitcast.201), channel_id=1, replica_groups=mesh['batch'=4,'seq'=2,'ch'=4] {'ch'}, use_global_device_ids=true, to_apply=%region_18.19 | all-reduce | flops 8192 | bytes 65536 | tf_op jit(solution)/shard_map/psum | solution.py:35
  677.9 5.5 convert_reduce_fusion.2
  684.8 3.0 collective-permute-start.4
  688.8 2.5 concatenate.25
  691.4 3.2 copy.69
  694.9 66.8 %all-gather.6.cloned.1.call-done = bf16[4,640,1152]{2,0,1:T(4,128)(2,1)} async-done(((bf16[4,160,1152]{2,0,1:T(4,128)(2,1)}), bf16[4,640,1152]{2,0,1:T(4,128)(2,1)}) %all-gather.6.cloned.1.call-update) | async-done | bytes 5898256 | tf_op jit(solution)/shard_map/all_gather | solution.py:129
  761.7 25.3 %fusion.110 = (bf16[4,640,1024]{2,0,1:T(4,128)(2,1)S(1)}, bf16[4,640,1024]{2,0,1:T(4,128)(2,1)S(1)}, bf16[4,640,1024]{2,0,1:T(4,128)(2,1)S(1)}, bf16[4,640,1024]{2,0,1:T(4,128)(2,1)S(1)}, bf16[4,640,1024]{2,0,1:T(4,128)(2,1)}) fusion(bf16[4,640,1152]{2,0,1:T(4,128)(2,1)} %all-gather.6.cloned.1.call-done), kind=kLoop, calls=%fused_computation.198 | loop fusion | bytes 52428800 | tf_op jit(solution)/shard_map/slice | solution.py:64
  787.0 8.6 fusion.28
  795.7 4.3 fusion.26
  800.0 4.1 bitcast_dynamic-update-slice_fusion
  804.1 4.2 fusion.24
  808.3 4.3 fusion.22
  812.6 18.1 %multiply_reduce_fusion.2 = (f32[160]{0:T(256)S(1)}, f32[4,1024]{1,0:T(4,128)S(1)}, f32[4,1024]{1,0:T(4,128)S(1)}, f32[160]{0:T(256)S(1)}, f32[4,160,1024]{2,1,0:T(8,128)}) fusion(f32[4,1024]{1,0:T(4,128)S(1)} %get-tuple-element.115, f32[4,1024]{1,0:T(4,128)S(1)} %get-tuple-element.114, f32[160]{0:T(256)S(1)} %copy-done.24, ...), kind=kOutput, calls=%fused_computation.96 | convolution fusion | flops 4248690176 | bytes 32550016 | tf_op jit(solution)/shard_map/sml,mc->scl/dot_general | solution.py:134
  830.8 15.4 %all-reduce.6 = (f32[4,1,1024]{2,0,1:T(4,128)S(1)}, f32[4,1,1024]{2,0,1:T(4,128)S(1)}) all-reduce(f32[4,1,1024]{2,0,1:T(4,128)S(1)} %bitcast.202, f32[4,1,1024]{2,0,1:T(4,128)S(1)} %bitcast.203), channel_id=1, replica_groups=mesh['batch'=4,'seq'=2,'ch'=4] {'ch'}, use_global_device_ids=true, to_apply=%region_22.23 | all-reduce | flops 8192 | bytes 65536 | tf_op jit(solution)/shard_map/psum | solution.py:35
  846.2 4.8 convert_reduce_fusion.3
  853.2 9.4 convolution_bitcast_fusion
  862.6 25.4 %copy.67 = f32[4,1280,1024]{2,0,1:T(4,128)} copy(f32[4,1280,1024]{1,2,0:T(8,128)} %convolution_bitcast_fusion) | data formatting | bytes 41943040 | tf_op jit(solution)/shard_map/shl,hd->sdl/transpose | solution.py:112
  888.9 8.5 convolution_bitcast_fusion.3
  897.4 12.0 fusion.74
  909.4 5.3 all-gather.8.cloned.1.call-done
  914.7 8.1 fusion.93
  923.9 12.3 fusion.17
  936.2 17.4 %all-reduce.5 = (f32[4,1,1024]{2,0,1:T(4,128)S(1)}, f32[4,1,1024]{2,0,1:T(4,128)S(1)}) all-reduce(f32[4,1,1024]{2,0,1:T(4,128)S(1)} %bitcast.198, f32[4,1,1024]{2,0,1:T(4,128)S(1)} %bitcast.199), channel_id=1, replica_groups=mesh['batch'=4,'seq'=2,'ch'=4] {'ch'}, use_global_device_ids=true, to_apply=%region_26.27 | all-reduce | flops 8192 | bytes 65536 | tf_op jit(solution)/shard_map/psum | solution.py:35
  953.7 340.3 %all-reduce.20.cloned.1.call-done = f32[4,1280,1024]{2,0,1:T(4,128)} async-done(((f32[4,1280,1024]{2,0,1:T(4,128)}), f32[4,1280,1024]{2,0,1:T(4,128)}) %all-reduce.20.cloned.1.call-update) | async-done | bytes 20971536
  1294.0 3.9 constant_dynamic-slice_fusion
  1299.7 6.9 convert_reduce_fusion.1
  1306.6 30.6 %all-reduce.3 = (f32[320]{0:T(512)}, f32[320]{0:T(512)}, f32[160]{0:T(256)}, f32[160]{0:T(256)}, f32[160]{0:T(256)}, /*index=5*/f32[160]{0:T(256)}, f32[160]{0:T(256)}, f32[160]{0:T(256)}, f32[320]{0:T(512)}) all-reduce(f32[320]{0:T(512)S(1)} %get-tuple-element.42, ...), channel_id=1, replica_groups=mesh['batch'=4,'seq'=2,'ch'=4] {'batch','seq'}, use_global_device_ids=true, to_apply=%region_28.29 | all-reduce | flops 1920 | bytes 15360 | tf_op jit(solution)/shard_map/psum | solution.py:159
  1337.2 50.5 %all-reduce.22.cloned.1.call-done = (f32[320,640]{1,0:T(8,128)}, f32[5,160,640]{2,1,0:T(8,128)}, f32[160,1280]{1,0:T(8,128)}) async-done(((f32[320,640]{1,0:T(8,128)}, f32[5,160,640]{2,1,0:T(8,128)}, f32[160,1280]{1,0:T(8,128)}), (f32[320,640]{1,0:T(8,128)}, f32[5,160,640]{2,1,0:T(8,128)}, f32[160,1280]{1,0:T(8,128)})) %all-reduce.22.cloned.1.call-update) | async-done | bytes 3686416 | tf_op jit(solution)/shard_map/psum | solution.py:159
  1389.9 3.0 copy.193
  (129 shorter events, 30.7 us)
Async XLA Ops:
  7.2 306.6 %copy-start = (bf16[5,160,640]{2,1,0:T(8,128)(2,1)S(1)}, bf16[5,160,640]{2,1,0:T(8,128)(2,1)}, u32[]{:S(2)}) copy-start(bf16[5,160,640]{2,1,0:T(8,128)(2,1)} %param.23) | copy-start | bytes 3072004
  7.2 20.4 %copy-start.28 = (f32[320]{0:T(512)S(1)}, f32[320]{0:T(512)}, u32[]{:S(2)}) copy-start(f32[320]{0:T(512)} %param.17) | copy-start | bytes 3844
  7.2 20.4 %copy-start.34 = (f32[320]{0:T(512)S(1)}, f32[320]{0:T(512)}, u32[]{:S(2)}) copy-start(f32[320]{0:T(512)} %param.18) | copy-start | bytes 3844
  7.2 261.1 %all-reduce.16.cloned.1.call-start = ((), (), s32[]{:S(2)}) async-start(), calls=%async_computation.3 | async-start | bytes 20971520
  27.6 14.7 %copy-start.18 = (f32[4,1024]{1,0:T(4,128)}, f32[4,1024]{1,0:T(4,128)S(1)}, u32[]{:S(2)}) copy-start(f32[4,1024]{1,0:T(4,128)S(1)} %get-tuple-element.116) | copy-start | bytes 49156
  27.6 14.7 %copy-start.20 = (f32[4,1024]{1,0:T(4,128)}, f32[4,1024]{1,0:T(4,128)S(1)}, u32[]{:S(2)}) copy-start(f32[4,1024]{1,0:T(4,128)S(1)} %get-tuple-element.117) | copy-start | bytes 49156
  27.7 16.2 %copy-start.15 = (bf16[320,640]{1,0:T(8,128)(2,1)S(1)}, bf16[320,640]{1,0:T(8,128)(2,1)}, u32[]{:S(2)}) copy-start(bf16[320,640]{1,0:T(8,128)(2,1)} %param.19) | copy-start | bytes 1228804
  42.3 1.5 copy-start.10
  62.4 5.1 copy-start.40
  62.5 480.2 %all-reduce.18.cloned.1.call-start = ((), (), s32[]{:S(2)}) async-start(), calls=%async_computation.4 | async-start | bytes 20971520
  63.2 235.7 %collective-permute-start.2 = (s32[4,64]{1,0:T(4,128)S(1)}, s32[4,64]{1,0:T(4,128)S(1)}, u32[]{:S(2)}, u32[]{:S(2)}) collective-permute-start(s32[4,64]{1,0:T(4,128)S(1)} %get-tuple-element.112), channel_id=1, source_target_pairs={{4,0},{5,1},{6,2},{7,3},{12,8},{13,9},{14,10},{15,11},{20,16},{21,... | collective-permute-start | bytes 3080 | tf_op jit(solution)/shard_map/ppermute | solution.py:21
  64.5 234.4 %collective-permute-start = (s32[4,64]{1,0:T(4,128)S(1)}, s32[4,64]{1,0:T(4,128)S(1)}, u32[]{:S(2)}, u32[]{:S(2)}) collective-permute-start(s32[4,64]{1,0:T(4,128)S(1)} %get-tuple-element.113), channel_id=1, source_target_pairs={{0,4},{1,5},{2,6},{3,7},{8,12},{9,13},{10,14},{11,15},{16,20},{17,... | collective-permute-start | bytes 3080 | tf_op jit(solution)/shard_map/ppermute | solution.py:20
  68.8 203.3 %copy-start.23 = (f32[160]{0:T(256)S(1)}, f32[160]{0:T(256)}, u32[]{:S(2)}) copy-start(f32[160]{0:T(256)} %param.20) | copy-start | bytes 1924
  270.6 1.5 copy-start.2
  272.1 17.2 %copy-start.26 = (f32[160]{0:T(256)S(1)}, f32[160]{0:T(256)}, u32[]{:S(2)}) copy-start(f32[160]{0:T(256)} %param.21) | copy-start | bytes 1924
  272.1 17.2 %copy-start.32 = (f32[160]{0:T(256)S(1)}, f32[160]{0:T(256)}, u32[]{:S(2)}) copy-start(f32[160]{0:T(256)} %param.22) | copy-start | bytes 1924
  297.6 2.9 collective-permute-start.1
  299.0 10.4 collective-permute-start.3
  300.5 1.7 copy-start.3
  311.1 2.7 copy-start.17
  335.8 314.4 %all-gather.4.cloned.1.call-start = ((), (), s32[]{:S(2)}) async-start(), calls=%async_computation | async-start | bytes 13107200 | tf_op jit(solution)/shard_map/all_gather | solution.py:115
  336.5 209.9 %copy-start.25 = (f32[160]{0:T(256)S(1)}, f32[160]{0:T(256)}, u32[]{:S(2)}) copy-start(f32[160]{0:T(256)} %param.24) | copy-start | bytes 1924
  336.5 425.2 %all-gather.6.cloned.1.call-start = ((), (), s32[]{:S(2)}) async-start(), calls=%async_computation.1 | async-start | bytes 7372800 | tf_op jit(solution)/shard_map/all_gather | solution.py:129
  544.9 1.5 copy-start.5
  546.4 18.2 %copy-start.30 = (f32[160]{0:T(256)S(1)}, f32[160]{0:T(256)}, u32[]{:S(2)}) copy-start(f32[160]{0:T(256)} %param.25) | copy-start | bytes 1924
  546.4 18.2 %copy-start.37 = (f32[160]{0:T(256)S(1)}, f32[160]{0:T(256)}, u32[]{:S(2)}) copy-start(f32[160]{0:T(256)} %param.26) | copy-start | bytes 1924
  564.7 85.5 %copy-start.13 = (bf16[160,1280]{1,0:T(8,128)(2,1)S(1)}, bf16[160,1280]{1,0:T(8,128)(2,1)}, u32[]{:S(2)}) copy-start(bf16[160,1280]{1,0:T(8,128)(2,1)} %param.27) | copy-start | bytes 1228804
  683.5 4.4 collective-permute-start.5
  684.8 4.1 collective-permute-start.4
  694.6 220.1 %all-gather.8.cloned.1.call-start = ((), (), s32[]{:S(2)}) async-start(), calls=%async_computation.2 | async-start | bytes 6553600 | tf_op jit(solution)/shard_map/all_gather | solution.py:148
  787.0 12.9 copy-start.7
  808.3 4.3 copy-start.4
  808.3 4.3 copy-start.24
  808.3 4.3 copy-start.27
  808.3 4.3 copy-start.33
  851.0 2.2 copy-start.8
  851.0 2.2 copy-start.14
  853.1 440.9 %all-reduce.20.cloned.1.call-start = ((), (), s32[]{:S(2)}) async-start(), calls=%async_computation.5 | async-start | bytes 41943040
  888.0 499.6 %all-reduce.22.cloned.1.call-start = ((), (), s32[]{:S(2)}) async-start(), calls=%async_computation.6 | async-start | bytes 7372800 | tf_op jit(solution)/shard_map/psum | solution.py:159
  953.7 344.3 %copy-start.36 = (f32[320]{0:T(512)S(1)}, f32[320]{0:T(512)}, u32[]{:S(2)}) copy-start(f32[320]{0:T(512)} %param.28) | copy-start | bytes 3844
  1294.0 4.0 copy-start.6
  1294.0 4.1 copy-start.9
  1294.0 5.6 copy-start.11
  1299.6 6.9 copy-start.31
  1299.6 6.9 copy-start.38
  1299.7 6.9 copy-start.39
  1387.6 5.2 copy-start.12
  1387.6 6.1 copy-start.1
  (6 other events, 6.3 us)
Sparse Core Ops, SparseCore 0:
  62.6 205.6 all-reduce.15
  335.9 206.6 all-reduce.17
  544.5 105.6 all-gather.3
  694.8 66.8 all-gather.5
  853.3 61.3 all-gather.7
  918.1 375.9 all-reduce.19
  1297.9 89.6 all-reduce.21
where the time goes:
time: 1410 us; the launch traced here: 1400 us
  waiting for transfers between devices  947 us (67%)
  blocking collectives  129 us (9%)
  local copies, waits for them, and re-layouts  115 us (8%)
  matrix products  95.6 us (7%)
  other arithmetic  86.6 us (6%)
  between operations  16.2 us (1%)
    unnamed x10, waiting for transfers between devices  747 us
    psum x6, blocking collectives, channel_sums(): return lax.psum((first, second), 'ch')  98.3 us
    all_gather x1, waiting for transfers between devices, local(): piece = lax.all_gather(cotangent, 'ch', axis=1, tiled=True)  76.4 us
    all_gather x1, waiting for transfers between devices, local(): piece = lax.all_gather(wide_grad, 'ch', axis=1, tiled=True)  66.8 us
    psum x1, waiting for transfers between devices, local(): lax.psum((grad_norm0_gain, grad_norm0_shift, grad_weight, grad_b_inner, g...  50.5 us
    psum x1, blocking collectives, local(): lax.psum((grad_norm0_gain, grad_norm0_shift, grad_weight, grad_b_inner, g...  30.6 us
    unnamed x90, local copies, waits for them, and re-layouts  30.3 us
  transfers between devices with their start and end apart: 13, of which 8 were waited for; matrix products, arithmetic and copies ran while one was open for 9% of the time, Pallas kernels for 0%

commit v1 on v0

v1 whole, which is shorter than its diff:
```python
import jax
import jax.numpy as jnp
from jax import lax
from jax.sharding import PartitionSpec as P

KERNEL_TAPS = 5
DILATION_SPACING = 32


EPSILON = 1e-05


def gelu_exact(values):
    return jax.nn.gelu(values, approximate=False)


def gelu_back(point, grad):
    return jax.vjp(gelu_exact, point)[1](grad)[0]


def normalize(values, gain, shift):
    center = jnp.mean(values, axis=1, keepdims=True)
    offset = values - center
    spread = jnp.mean(offset * offset, axis=1, keepdims=True)
    scale = lax.rsqrt(spread + EPSILON)
    unit = offset * scale
    return (unit * gain[:, None] + shift[:, None], unit, scale)


def normalize_back(grad, unit, scale, gain):
    scaled = grad * gain[:, None]
    first = jnp.mean(scaled, axis=1, keepdims=True)
    second = jnp.mean(scaled * unit, axis=1, keepdims=True)
    return scale * (scaled - first - unit * second)


def neighbour_pairs(seqs, nch, q_count):
    pairs = []
    for s in range(seqs):
        for c in range(nch):
            q = c % q_count
            if q < q_count - 1:
                pairs.append((s * nch + c, s * nch + c + 1))
            elif s < seqs - 1:
                pairs.append((s * nch + c, (s + 1) * nch + c - (q_count - 1)))
    return pairs


def extended(x, width, pairs):
    down = [(j, i) for i, j in pairs]
    length = x.shape[-1]
    before = lax.ppermute(x[..., length - width :], ("seq", "ch"), pairs)
    after = lax.ppermute(x[..., :width], ("seq", "ch"), down)
    return jnp.concatenate([before, x, after], axis=-1)


def shifted_taps(wide, wide_ids, own_ids, offsets, border):
    length = own_ids.shape[-1]
    pieces = []
    for offset in offsets:
        lower = border + offset
        shifted = wide[:, :, lower : lower + length]
        matching = wide_ids[:, lower : lower + length] == own_ids
        pieces.append(jnp.where(matching[:, None, :], shifted, jnp.zeros_like(shifted)))
    return jnp.concatenate(pieces, axis=1)


def to_positions(x, nch, q_count):
    rows, width, length = x.shape
    if q_count > 1:
        x = x.reshape(rows, width, q_count, length // q_count).transpose(0, 2, 1, 3)
        x = x.reshape(rows * q_count, width, length // q_count)
    return lax.all_to_all(x, "ch", 0, 1, tiled=True)


def to_channels(x, nch, q_count, rows):
    x = lax.all_to_all(x, "ch", 1, 0, tiled=True)
    if q_count > 1:
        _, width, part = x.shape
        x = x.reshape(rows, q_count, width, part).transpose(0, 2, 1, 3).reshape(rows, width, q_count * part)
    return x


def local(
    inputs,
    segment_ids,
    norm0_gain,
    norm0_shift,
    w_inner,
    b_inner,
    norm1_gain,
    norm1_shift,
    w_conv,
    b_conv,
    norm2_gain,
    norm2_shift,
    w_outer,
    b_outer,
    cotangent,
):
    nch = lax.axis_size("ch")
    seqs = lax.axis_size("seq")
    batches = lax.axis_size("batch")
    rows, dloc, length = inputs.shape
    hloc = w_conv.shape[1]
    hid = hloc * nch
    dim = dloc * nch
    if rows % nch == 0:
        q_count = 1
    else:
        q_count = nch // rows
    part = length // q_count
    border = 2 * DILATION_SPACING
    offsets = [(k - KERNEL_TAPS // 2) * DILATION_SPACING for k in range(KERNEL_TAPS)]
    back_offsets = [-o for o in offsets]
    pairs = neighbour_pairs(seqs, nch, q_count)
    me = lax.axis_index("ch")

    smalls = [norm0_gain, norm0_shift, b_inner, norm1_gain, norm1_shift, b_conv, norm2_gain, norm2_shift, b_outer]
    small_all = lax.all_gather(jnp.concatenate(smalls), "ch", axis=0, tiled=False)
    cut = 0
    full = []
    for s in smalls:
        n = s.shape[0]
        full.append(small_all[:, cut : cut + n].reshape(n * nch))
        cut += n
    g0, s0, b_in, g1, s1, b_cv, g2, s2, b_out = full
    packed = jnp.concatenate([w_inner.reshape(-1), w_conv.reshape(-1), w_outer.reshape(-1)])
    packed_all = lax.all_gather(packed.reshape(1, -1, 128), "ch", axis=0, tiled=True).reshape(nch, -1)
    n_in, n_cv = w_inner.size, w_conv.size
    w_in = packed_all[:, :n_in].reshape(dim, hid)
    w_cv = (
        packed_all[:, n_in : n_in + n_cv]
        .reshape(nch, KERNEL_TAPS, hloc, hid)
        .transpose(1, 0, 2, 3)
        .reshape(KERNEL_TAPS, hid, hid)
    )
    w_out = packed_all[:, n_in + n_cv :].reshape(hid, dim)

    x = to_positions(inputs, nch, q_count)
    cot = to_positions(cotangent, nch, q_count)
    prow = x.shape[0]
    if q_count == 1:
        ids = lax.dynamic_slice_in_dim(segment_ids, me * prow, prow, axis=0)
    else:
        ids = lax.dynamic_slice_in_dim(segment_ids, me // q_count, 1, axis=0)
        ids = lax.dynamic_slice_in_dim(ids, (me % q_count) * part, part, axis=1)
    own_ids = ids + 1
    wide_ids = extended(own_ids, border, pairs)

    residual = x.astype(jnp.float32)
    normed0, unit0, scale0 = normalize(residual, g0, s0)
    hidden0 = gelu_exact(normed0).astype(jnp.bfloat16)
    inner = jnp.einsum("dh,rdl->rhl", w_in, hidden0, preferred_element_type=jnp.float32) + b_in[:, None]
    normed1, unit1, scale1 = normalize(inner, g1, s1)
    hidden1 = gelu_exact(normed1).astype(jnp.bfloat16)
    wide_hidden = extended(hidden1, border, pairs)
    taps = shifted_taps(wide_hidden, wide_ids, own_ids, offsets, border)
    kernel_flat = w_cv.reshape(KERNEL_TAPS * hid, hid)
    mixed = jnp.einsum("co,rcl->rol", kernel_flat, taps, preferred_element_type=jnp.float32) + b_cv[:, None]
    normed2, unit2, scale2 = normalize(mixed, g2, s2)
    hidden2 = gelu_exact(normed2).astype(jnp.bfloat16)
    branch = jnp.einsum("hd,rhl->rdl", w_out, hidden2, preferred_element_type=jnp.float32)
    output = (residual + branch + b_out[:, None]).astype(jnp.bfloat16)

    grad_b_outer = jnp.sum(cot.astype(jnp.float32), axis=(0, 2))
    grad_w_outer = jnp.einsum("rhl,rdl->hd", hidden2, cot, preferred_element_type=jnp.float32)
    grad_hidden2 = jnp.einsum("hd,rdl->rhl", w_out, cot, preferred_element_type=jnp.float32)
    grad_normed2 = gelu_back(normed2, grad_hidden2)
    grad_norm2_gain = jnp.sum(grad_normed2 * unit2, axis=(0, 2))
    grad_norm2_shift = jnp.sum(grad_normed2, axis=(0, 2))
    grad_mixed = normalize_back(grad_normed2, unit2, scale2, g2).astype(jnp.bfloat16)
    grad_b_conv = jnp.sum(grad_mixed.astype(jnp.float32), axis=(0, 2))
    grad_w_conv = jnp.einsum("rcl,rol->co", taps, grad_mixed, preferred_element_type=jnp.float32).reshape(
        KERNEL_TAPS, hid, hid
    )
    wide_grad = extended(grad_mixed, border, pairs)
    back_taps = shifted_taps(wide_grad, wide_ids, own_ids, back_offsets, border)
    kernel_back = jnp.transpose(w_cv, (0, 2, 1)).reshape(KERNEL_TAPS * hid, hid)
    grad_hidden1 = jnp.einsum("oc,rol->rcl", kernel_back, back_taps, preferred_element_type=jnp.float32)
    grad_normed1 = gelu_back(normed1, grad_hidden1)
    grad_norm1_gain = jnp.sum(grad_normed1 * unit1, axis=(0, 2))
    grad_norm1_shift = jnp.sum(grad_normed1, axis=(0, 2))
    grad_inner = normalize_back(grad_normed1, unit1, scale1, g1).astype(jnp.bfloat16)
    grad_b_inner = jnp.sum(grad_inner.astype(jnp.float32), axis=(0, 2))
    grad_w_inner = jnp.einsum("rdl,rhl->dh", hidden0, grad_inner, preferred_element_type=jnp.float32)
    grad_hidden0 = jnp.einsum("dh,rhl->rdl", w_in, grad_inner, preferred_element_type=jnp.float32)
    grad_normed0 = gelu_back(normed0, grad_hidden0)
    grad_norm0_gain = jnp.sum(grad_normed0 * unit0, axis=(0, 2))
    grad_norm0_shift = jnp.sum(grad_normed0, axis=(0, 2))
    input_grad = (cot.astype(jnp.float32) + normalize_back(grad_normed0, unit0, scale0, g0)).astype(jnp.bfloat16)

    output = to_channels(output, nch, q_count, rows)
    input_grad = to_channels(input_grad, nch, q_count, rows)

    grads = [
        grad_norm0_gain,
        grad_norm0_shift,
        grad_w_inner,
        grad_b_inner,
        grad_norm1_gain,
        grad_norm1_shift,
        grad_w_conv.transpose(1, 0, 2),
        grad_b_conv,
        grad_norm2_gain,
        grad_norm2_shift,
        grad_w_outer,
        grad_b_outer,
    ]
    flat = [g.reshape(nch, -1) for g in grads]
    sizes = [f.shape[1] for f in flat]
    stack = jnp.concatenate(flat, axis=1)
    total = stack.shape[1]
    lanes = 128
    spread = seqs * batches * 8 * lanes
    padded = -(-total // spread) * spread
    if padded != total:
        stack = jnp.pad(stack, ((0, 0), (0, padded - total)))
    stack = stack.reshape(nch, padded // lanes, lanes)
    stack = lax.psum_scatter(stack, "seq", scatter_dimension=1, tiled=True)
    stack = lax.psum_scatter(stack, "batch", scatter_dimension=1, tiled=True)
    stack = lax.psum_scatter(stack, "ch", scatter_dimension=0, tiled=True)
    stack = lax.all_gather(stack, ("seq", "batch"), axis=1, tiled=True).reshape(padded)[:total]
    shard_shapes = [
        norm0_gain.shape,
        norm0_shift.shape,
        w_inner.shape,
        b_inner.shape,
        norm1_gain.shape,
        norm1_shift.shape,
        (hloc, KERNEL_TAPS, hid),
        b_conv.shape,
        norm2_gain.shape,
        norm2_shift.shape,
        w_outer.shape,
        b_outer.shape,
    ]
    outs = []
    cut = 0
    for n, shape in zip(sizes, shard_shapes):
        outs.append(stack[cut : cut + n].reshape(shape))
        cut += n
    outs[6] = outs[6].transpose(1, 0, 2)
    return (output, input_grad, *outs)


def solution(mesh):
    return jax.shard_map(
        local,
        mesh=mesh,
        in_specs=(
            P("batch", "ch", "seq"),
            P("batch", "seq"),
            P("ch"),
            P("ch"),
            P("ch", None),
            P("ch"),
            P("ch"),
            P("ch"),
            P(None, "ch", None),
            P("ch"),
            P("ch"),
            P("ch"),
            P("ch", None),
            P("ch"),
            P("batch", "ch", "seq"),
        ),
        out_specs=(
            P("batch", "ch", "seq"),
            P("batch", "ch", "seq"),
            P("ch"),
            P("ch"),
            P("ch", None),
            P("ch"),
            P("ch"),
            P("ch"),
            P(None, "ch", None),
            P("ch"),
            P("ch"),
            P("ch"),
            P("ch", None),
            P("ch"),
        ),
        check_vma=False,
    )
```

time: 1410 us -> 824 us (0.58)
  waiting for transfers between devices: 947 us -> 264 us
  local copies, waits for them, and re-layouts: 115 us -> 272 us
  blocking collectives: 129 us -> 49.7 us
  starting transfers between devices: 12 us -> 29.8 us
    unnamed x10 -> x6, waiting for transfers between devices: 747 us -> 37.6 us
    reduce_scatter x0 -> x2, waiting for transfers between devices: none -> 157 us  [the longest x1 132 us: local(): stack = lax.psum_scatter(stack, 'batch', scatter_dimension=1, tiled=True)]
    unnamed x90 -> x88, local copies, waits for them, and re-layouts: 30.3 us -> 160 us
    psum x7 -> x0, blocking collectives: 129 us -> none  [the longest x6 98.3 us: channel_sums(): return lax.psum((first, second), 'ch')]
    all_gather x3 -> x2, waiting for transfers between devices: 149 us -> 48.9 us  [the longest x1 48.9 us: local(): lax.all_gather(packed.reshape(1, -1, 128), 'ch', axis=0, tiled=True)]
    psum x1 -> x0, waiting for transfers between devices: 50.5 us -> none  [local(): lax.psum((grad_norm0_gain, grad_norm0_shift, grad_weight, grad_b_inner, g...]
    all_gather x0 -> x1, blocking collectives: none -> 49.7 us  [local(): lax.all_gather(jnp.concatenate(smalls), 'ch', axis=0, tiled=False)]
    reshape x0 -> x19, local copies, waits for them, and re-layouts: none -> 36.9 us  [the longest x11 21.3 us: local(): flat = [g.reshape(nch, -1) for g in grads]]
  transfers between devices with their start and end apart: 13 -> 15, of which waited for: 8 -> 5; matrix products, arithmetic and copies ran while one was open for 9% -> 28% of each run, Pallas kernels for 0% -> 0%
where the time goes in v1:
time: 824 us; the launch traced here: 816 us
  local copies, waits for them, and re-layouts  272 us (33%)
  waiting for transfers between devices  264 us (32%)
  matrix products  95.8 us (12%)
  other arithmetic  90.3 us (11%)
  blocking collectives  49.7 us (6%)
  starting transfers between devices  29.8 us (4%)
  between operations  14.7 us (2%)
    unnamed x88, local copies, waits for them, and re-layouts  160 us
    reduce_scatter x1, waiting for transfers between devices, local(): stack = lax.psum_scatter(stack, 'batch', scatter_dimension=1, tiled=True)  132 us
    all_gather x1, blocking collectives, local(): lax.all_gather(jnp.concatenate(smalls), 'ch', axis=0, tiled=False)  49.7 us
    all_gather x1, waiting for transfers between devices, local(): lax.all_gather(packed.reshape(1, -1, 128), 'ch', axis=0, tiled=True)  48.9 us
    unnamed x10, other arithmetic  46 us
    unnamed x6, waiting for transfers between devices  37.6 us
    reduce_scatter x1, waiting for transfers between devices, local(): stack = lax.psum_scatter(stack, 'seq', scatter_dimension=1, tiled=True)  24.9 us
    reshape x11, local copies, waits for them, and re-layouts, local(): flat = [g.reshape(nch, -1) for g in grads]  21.3 us
  transfers between devices with their start and end apart: 15, of which 5 were waited for; matrix products, arithmetic and copies ran while one was open for 28% of the time, Pallas kernels for 0%

profile of v1, /device:TPU:0, one launch (start us, length us, event | category | flops | bytes accessed | tf_op | source)
XLA Modules:
  0.0 816.4 jit_solution(5555885793643184578)
XLA Ops:
  13.4 5.3 all-to-all-start
  22.4 49.7 %all-gather.1 = f32[4,1,1920]{2,1,0:T(1,128)S(1)} all-gather(f32[1,1,1920]{2,1,0:T(1,128)S(1)} %reshape.1500), channel_id=2, replica_groups=mesh['batch'=4,'seq'=2,'ch'=4] {'ch'}, dimensions={0}, use_global_device_ids=true | all-gather | bytes 38400 | tf_op jit(solution)/shard_map/all_gather | solution.py:120
  73.7 4.8 all-to-all-start.2
  81.5 14.6 %fusion.6 = bf16[1,1280,1,1,1,1,1024]{6,1,5,4,3,2,0:T(8,128)(2,1)} fusion(f32[1,1280,1,1,1,1,1024]{6,1,5,4,3,2,0:T(8,128)S(1)} %bitcast.270, f32[1280]{0:T(1024)S(1)} %add.153, f32[1280]{0:T(1024)S(1)} %mul.431, f32[1024]{0:T(1024)S(1)} %add_rsqrt_fusion.2, f32[1024]{0:T(1024)S(1)} %broadcast_multiply_fusion.8), kind=kLoop, calls=%fused_computation.11 | loop fusion | flops 90439680 | bytes 7882752 | tf_op jit(solution)/shard_map/convert_element_type | solution.py:153
  96.1 48.9 %all-gather.5.cloned.1.call-done = bf16[4,7200,128]{2,1,0:T(8,128)(2,1)} async-done(((bf16[1,7200,128]{2,1,0:T(8,128)(2,1)}), bf16[4,7200,128]{2,1,0:T(8,128)(2,1)}) %all-gather.5.cloned.1.call-update) | async-done | bytes 7372816 | tf_op jit(solution)/shard_map/all_gather | solution.py:129
  145.0 26.1 %copy.86 = bf16[1,4,7200,128]{3,1,2,0:T(4,128)(2,1)S(1)} copy(bf16[1,4,7200,128]{3,2,1,0:T(8,128)(2,1)} %bitcast.283) | data formatting | bytes 14745600
  178.4 4.5 fusion.72
  183.5 7.3 multiply_convert_fusion.1
  196.9 5.9 copy.61
  202.8 3.6 slice.212
  209.3 4.1 reshape.1474
  214.7 7.9 copy.66
  226.9 8.0 constant_dynamic-update-slice_fusion
  237.8 9.6 %copy.69 = bf16[1,3200,1024]{2,1,0:T(8,128)(2,1)} copy(bf16[1,3200,1024]{1,2,0:T(8,128)(2,1)} %fusion.97) | data formatting | bytes 13107200 | tf_op jit(solution)/shard_map/concatenate | solution.py:65
  247.4 9.1 %fusion.74 = (f32[1024]{0:T(1024)S(1)}, f32[1024,640]{1,0:T(8,128)S(1)}) fusion(f32[640]{0:T(1024)S(1)} %add.163, bf16[3200,640]{1,0:T(8,128)(2,1)} %bitcast.279, bf16[1,3200,1024]{1,2,0:T(8,128)(2,1)} %fusion.97), kind=kOutput, calls=%fused_computation.146 | convolution fusion | flops 4195613696 | bytes 13277696 | tf_op jit(solution)/shard_map/co,rcl->rol/dot_general | solution.py:160
  257.1 11.8 %fusion.105 = f32[640,1280]{1,0:T(8,128)} fusion(bf16[1280,1024]{1,0:T(8,128)(2,1)} %bitcast.15, f32[640]{0:T(1024)S(1)} %add.167, f32[640]{0:T(1024)S(1)} %mul.451, f32[1024]{0:T(1024)S(1)} %add_rsqrt_fusion, f32[1024]{0:T(1024)S(1)} %broadcast_multiply_fusion.4, f32[640]{0:T(1024)S(1)} %add.163, f32[1024,640]{1,0:T(8,128)S(1)} %get-tuple-element.121), kind=kOutput, calls=%fused_computation.218 | convolution fusion | flops 1723596800 | bytes 8535552 | tf_op jit(solution)/shard_map/rhl,rdl->hd/dot_general | solution.py:167
  268.9 12.2 %fusion.50 = (f32[640]{0:T(1024)S(1)}, f32[1024]{0:T(1024)S(1)}, f32[1024]{0:T(1024)S(1)}, f32[640]{0:T(1024)S(1)}, f32[1,640,1024]{1,2,0:T(8,128)}) fusion(f32[1024]{0:T(1024)S(1)} %add_rsqrt_fusion, f32[1024]{0:T(1024)S(1)} %broadcast_multiply_fusion.4, f32[640]{0:T(1024)S(1)} %add.163, f32[1024,640]{1,0:T(8,128)S(1)} %get-tuple-element.121, ...), kind=kOutput, calls=%fused_computation.93 | convolution fusion | flops 1732113152 | bytes 9531904 | tf_op jit(solution)/shard_map/hd,rdl->rhl/dot_general | solution.py:168
  284.4 5.2 reshape.1491
  294.0 7.8 convolution_bitcast_fusion
  301.8 9.7 %copy.71 = f32[640,5,640]{2,1,0:T(8,128)} copy(f32[640,5,640]{2,0,1:T(8,128)S(1)} %convolution_bitcast_fusion) | data formatting | bytes 16384000 | tf_op jit(solution)/shard_map/transpose | solution.py:203
  311.5 12.0 %reshape.1487 = f32[4,512000]{1,0:T(4,128)} reshape(f32[640,5,640]{2,1,0:T(8,128)} %copy.71) | data formatting | bytes 16384000 | tf_op jit(solution)/shard_map/reshape | solution.py:210
  327.3 13.4 %fusion.56 = (f32[640]{0:T(1024)S(1)}, f32[1024]{0:T(1024)S(1)}, f32[1024]{0:T(1024)S(1)}, f32[640]{0:T(1024)S(1)}, f32[1,640,1024]{1,2,0:T(8,128)}) fusion(f32[1024]{0:T(1024)S(1)} %add_rsqrt_fusion.1, f32[1024]{0:T(1024)S(1)} %broadcast_multiply_fusion.5, f32[640]{0:T(1024)S(1)} %add.156, f32[1024,640]{1,0:T(8,128)S(1)} %copy-done.2, f32[640]{0:T(1024)S(1)} %mul.441, ...), kind=kOutput, calls=%fused_computation.104 | convolution fusion | flops 4248695808 | bytes 15921664 | tf_op jit(solution)/shard_map/oc,rol->rcl/dot_general | solution.py:180
  340.8 3.3 convert_reduce_fusion.2
  344.2 6.0 fusion.57
  350.2 3.5 reshape.1482
  353.7 19.2 %multiply_reduce_fusion = (f32[1280]{0:T(1024)S(1)}, f32[1024]{0:T(1024)S(1)}, f32[1024]{0:T(1024)S(1)}, f32[1280]{0:T(1024)S(1)}, f32[1,1280,1024]{1,2,0:T(8,128)}) fusion(f32[1,1280,1024]{1,2,0:T(8,128)} %copy.61, f32[1024]{0:T(1024)S(1)} %copy-done.15, f32[1024]{0:T(1024)S(1)} %copy-done.17, f32[1280]{0:T(1024)S(1)} %copy-done.13, ...), kind=kOutput, calls=%fused_computation.24 | convolution fusion | flops 1785196032 | bytes 13471744 | tf_op jit(solution)/shard_map/dh,rhl->rdl/dot_general | solution.py:187
  381.9 43.2 %dynamic-update-slice.6 = f32[4,923520]{1,0:T(4,128)} dynamic-update-slice(f32[4,923520]{1,0:T(4,128)} %dynamic-update-slice.5, f32[4,512000]{1,0:T(4,128)} %reshape.1487, s32[]{} %constant.29, s32[]{} %constant.35) | dynamic-update-slice | bytes 16384004
  429.5 17.2 %dynamic-update-slice.10 = f32[4,923520]{1,0:T(4,128)} dynamic-update-slice(f32[4,923520]{1,0:T(4,128)} %dynamic-update-slice.9, f32[4,204800]{1,0:T(4,128)S(1)} %copy-done.7, s32[]{} %constant.29, s32[]{} %constant.146) | dynamic-update-slice | bytes 6553604
  448.1 12.8 %pad_bitcast_fusion = f32[1,4,7232,128]{3,1,2,0:T(4,128)} fusion(f32[4,923520]{1,0:T(4,128)} %dynamic-update-slice.11), kind=kLoop, calls=%fused_computation.1 | loop fusion | bytes 29587456
  460.9 11.4 %copy.85 = f32[1,4,7232,128]{3,2,1,0:T(8,128)} copy(f32[1,4,7232,128]{3,1,2,0:T(4,128)} %pad_bitcast_fusion) | data formatting | bytes 29622272
  472.3 24.9 %reduce-scatter.6.cloned.1.call-done = f32[4,3616,128]{2,1,0:T(8,128)} async-done(((f32[4,7232,128]{2,1,0:T(8,128)}), f32[4,3616,128]{2,1,0:T(8,128)}) %reduce-scatter.6.cloned.1.call-update) | async-done | bytes 7405584 | tf_op jit(solution)/shard_map/reduce_scatter | solution.py:220
  497.3 132.5 %reduce-scatter.8.cloned.1.call-done = f32[4,904,128]{2,1,0:T(8,128)} async-done(((f32[4,3616,128]{2,1,0:T(8,128)}), f32[4,904,128]{2,1,0:T(8,128)}) %reduce-scatter.8.cloned.1.call-update) | async-done | bytes 1851408 | tf_op jit(solution)/shard_map/reduce_scatter | solution.py:221
  629.9 37.5 %reduce-scatter.10.cloned.1.call-done = f32[1,904,128]{2,1,0:T(8,128)} async-done(((f32[4,904,128]{2,1,0:T(8,128)}), f32[1,904,128]{2,1,0:T(8,128)}) %reduce-scatter.10.cloned.1.call-update) | async-done | bytes 462864
  667.5 11.7 %fusion.12 = bf16[1,1280,1024]{1,2,0:T(8,128)(2,1)} fusion(f32[1,1280,1024]{1,2,0:T(8,128)} %copy.61, bf16[640,1280]{1,0:T(8,128)(2,1)} %reshape.1474, f32[1280]{0:T(1024)S(1)} %add.171, f32[640]{0:T(1024)S(1)} %add.167, f32[640]{0:T(1024)S(1)} %mul.451, f32[1024]{0:T(1024)S(1)} %add_rsqrt_fusion, f32[1024]{0:T(1024)S(1)} %broadcast_multiply_fusion.4, ...), kind=kOutput, calls=%fused_computation.18 | convolution fusion | flops 1727528960 | bytes 12145152 | tf_op jit(solution)/shard_map/hd,rhl->rdl/dot_general | solution.py:163
  679.2 11.6 %copy.62 = bf16[1,1280,1024]{2,0,1:T(2,128)(2,1)} copy(bf16[1,1280,1024]{1,2,0:T(8,128)(2,1)} %fusion.12) | data formatting | bytes 5242880 | tf_op jit(solution)/shard_map/convert_element_type | solution.py:164
  691.3 15.6 %reduce.29 = bf16[1280,1024]{1,0:T(8,128)(2,1)S(1)} reduce(bf16[1280,1,1024]{2,1,0:T(2,128)(2,1)} %bitcast.274, bf16[]{:T(256)} %broadcast.2394), dimensions={1}, to_apply=%bitcast.237.reduce_sub_computation | reduce | bytes 5242882
  710.0 4.6 all-to-all-start.1
  714.6 4.9 copy.67
  719.5 6.4 add_convert_fusion
  725.9 8.3 %copy.68 = bf16[1,1280,1024]{2,0,1:T(2,128)(2,1)} copy(bf16[1,1280,1024]{1,2,0:T(8,128)(2,1)S(1)} %add_convert_fusion) | data formatting | bytes 5242880 | tf_op jit(solution)/shard_map/convert_element_type | solution.py:191
  734.2 15.6 %reduce.30 = bf16[1280,1024]{1,0:T(8,128)(2,1)S(1)} reduce(bf16[1280,1,1024]{2,1,0:T(2,128)(2,1)} %bitcast.275, bf16[]{:T(256)} %broadcast.2394), dimensions={1}, to_apply=%bitcast.239.reduce_sub_computation | reduce | bytes 5242882
  749.7 3.2 reshape.1511
  753.0 4.4 all-to-all-start.3
  757.4 5.5 reshape.1510
  762.9 5.0 copy.77
  767.9 19.7 %all-to-all-done.3 = bf16[4,2,163840]{2,1,0:T(2,128)(2,1)S(1)} async-done(((bf16[4,2,163840]{2,1,0:T(2,128)(2,1)}), bf16[4,2,163840]{2,1,0:T(2,128)(2,1)S(1)}, u32[]{:S(2)}, u32[]{:S(2)}) %all-to-all-start.3) | async-done | bytes 2621472 | tf_op jit(solution)/shard_map/all_to_all | solution.py:77
  787.5 3.8 reshape.1512
  791.4 5.0 copy.78
  (173 shorter events, 83.6 us)
Async XLA Ops:
  7.2 137.8 %all-gather.5.cloned.1.call-start = ((), (), s32[]{:S(2)}) async-start(), calls=%async_computation.7 | async-start | bytes 9216000 | tf_op jit(solution)/shard_map/all_gather | solution.py:129
  13.2 9.0 %copy-start.22 = (f32[320]{0:T(512)S(1)}, f32[320]{0:T(512)}, u32[]{:S(2)}) copy-start(f32[320]{0:T(512)} %param.17) | copy-start | bytes 3844
  13.3 9.0 %copy-start.23 = (f32[320]{0:T(512)S(1)}, f32[320]{0:T(512)}, u32[]{:S(2)}) copy-start(f32[320]{0:T(512)} %param.18) | copy-start | bytes 3844
  13.3 9.0 %copy-start.24 = (f32[320]{0:T(512)S(1)}, f32[320]{0:T(512)}, u32[]{:S(2)}) copy-start(f32[320]{0:T(512)} %param.28) | copy-start | bytes 3844
  13.3 9.0 %copy-start.25 = (f32[160]{0:T(256)S(1)}, f32[160]{0:T(256)}, u32[]{:S(2)}) copy-start(f32[160]{0:T(256)} %param.20) | copy-start | bytes 1924
  13.3 9.0 %copy-start.26 = (f32[160]{0:T(256)S(1)}, f32[160]{0:T(256)}, u32[]{:S(2)}) copy-start(f32[160]{0:T(256)} %param.21) | copy-start | bytes 1924
  13.3 9.0 %copy-start.27 = (f32[160]{0:T(256)S(1)}, f32[160]{0:T(256)}, u32[]{:S(2)}) copy-start(f32[160]{0:T(256)} %param.22) | copy-start | bytes 1924
  13.3 9.0 %copy-start.28 = (f32[160]{0:T(256)S(1)}, f32[160]{0:T(256)}, u32[]{:S(2)}) copy-start(f32[160]{0:T(256)} %param.24) | copy-start | bytes 1924
  13.3 9.0 %copy-start.29 = (f32[160]{0:T(256)S(1)}, f32[160]{0:T(256)}, u32[]{:S(2)}) copy-start(f32[160]{0:T(256)} %param.25) | copy-start | bytes 1924
  13.3 9.0 %copy-start.30 = (f32[160]{0:T(256)S(1)}, f32[160]{0:T(256)}, u32[]{:S(2)}) copy-start(f32[160]{0:T(256)} %param.26) | copy-start | bytes 1924
  13.4 60.4 %all-to-all-start = ((bf16[4,320,1024]{2,1,0:T(8,128)(2,1)}), bf16[4,320,1024]{2,1,0:T(8,128)(2,1)S(1)}, u32[]{:S(2)}, u32[]{:S(2)}) async-start(bf16[4,320,1024]{2,1,0:T(8,128)(2,1)} %param.15), calls=%async_computation | async-start | bytes 5242880 | tf_op jit(solution)/shard_map/all_to_all | solution.py:73
  19.5 54.1 %collective-permute-start = (s32[1,64]{1,0:T(1,128)S(1)}, s32[1,64]{1,0:T(1,128)S(1)}, u32[]{:S(2)}, u32[]{:S(2)}) collective-permute-start(s32[1,64]{1,0:T(1,128)S(1)} %get-tuple-element.116), channel_id=1, source_target_pairs={{0,4},{1,5},{2,6},{3,7},{8,12},{9,13},{10,14},{11,15},{16,20},{17,... | collective-permute-start | bytes 776 | tf_op jit(solution)/shard_map/ppermute | solution.py:52
  20.9 52.6 %collective-permute-start.2 = (s32[1,64]{1,0:T(1,128)S(1)}, s32[1,64]{1,0:T(1,128)S(1)}, u32[]{:S(2)}, u32[]{:S(2)}) collective-permute-start(s32[1,64]{1,0:T(1,128)S(1)} %get-tuple-element.117), channel_id=1, source_target_pairs={{4,0},{5,1},{6,2},{7,3},{12,8},{13,9},{14,10},{15,11},{20,16},{21,... | collective-permute-start | bytes 776 | tf_op jit(solution)/shard_map/ppermute | solution.py:53
  73.1 7.3 copy-start.12
  73.6 6.9 copy-start.18
  73.7 120.4 %all-to-all-start.2 = ((bf16[4,320,1024]{2,1,0:T(8,128)(2,1)}), bf16[4,320,1024]{2,1,0:T(8,128)(2,1)}, u32[]{:S(2)}, u32[]{:S(2)}) async-start(bf16[4,320,1024]{2,1,0:T(8,128)(2,1)} %param.29), calls=%async_computation.2 | async-start | bytes 5242880 | tf_op jit(solution)/shard_map/all_to_all | solution.py:73
  78.5 418.8 %reduce-scatter.6.cloned.1.call-start = ((), (), s32[]{:S(2)}) async-start(), calls=%async_computation.8 | async-start | bytes 22216704 | tf_op jit(solution)/shard_map/reduce_scatter | solution.py:220
  79.2 2.3 copy-start
  79.6 16.4 %copy-start.14 = (f32[1024]{0:T(1024)}, f32[1024]{0:T(1024)S(1)}, u32[]{:S(2)}) copy-start(f32[1024]{0:T(1024)S(1)} %broadcast_multiply_fusion.8) | copy-start | bytes 12292
  80.4 15.6 %copy-start.16 = (f32[1024]{0:T(1024)}, f32[1024]{0:T(1024)S(1)}, u32[]{:S(2)}) copy-start(f32[1024]{0:T(1024)S(1)} %add_rsqrt_fusion.2) | copy-start | bytes 12292
  171.0 3.0 copy-start.6
  182.9 44.0 %copy-start.1 = (f32[1024,640]{1,0:T(8,128)}, f32[1024,640]{1,0:T(8,128)S(1)}, u32[]{:S(2)}) copy-start(f32[1024,640]{1,0:T(8,128)S(1)} %get-tuple-element.119) | copy-start | bytes 7864324
  190.8 1.1 copy-start.4
  191.8 30.7 %collective-permute-start.1 = (bf16[1,640,64]{1,2,0:T(8,128)(2,1)S(1)}, bf16[1,640,64]{1,2,0:T(8,128)(2,1)S(1)}, u32[]{:S(2)}, u32[]{:S(2)}) collective-permute-start(bf16[1,640,64]{1,2,0:T(8,128)(2,1)S(1)} %get-tuple-element.106), channel_id=1, source_target_pairs={{0,4},{1,5},{2,6},{3,7},{8,12},{9,13},{10,14},{11,15},{16,20},{17,... | collective-permute-start | bytes 245768 | tf_op jit(solution)/shard_map/ppermute | solution.py:52
  213.4 21.5 %collective-permute-start.3 = (bf16[1,640,64]{1,2,0:T(8,128)(2,1)S(1)}, bf16[1,640,64]{1,2,0:T(8,128)(2,1)S(1)}, u32[]{:S(2)}, u32[]{:S(2)}) collective-permute-start(bf16[1,640,64]{1,2,0:T(8,128)(2,1)S(1)} %get-tuple-element.105), channel_id=1, source_target_pairs={{4,0},{5,1},{6,2},{7,3},{12,8},{13,9},{14,10},{15,11},{20,16},{21,... | collective-permute-start | bytes 245768 | tf_op jit(solution)/shard_map/ppermute | solution.py:53
  222.6 2.9 copy-start.5
  256.5 12.4 %copy-start.8 = (f32[1024,640]{1,0:T(8,128)}, f32[1024,640]{1,0:T(8,128)S(1)}, u32[]{:S(2)}) copy-start(f32[1024,640]{1,0:T(8,128)S(1)} %get-tuple-element.121) | copy-start | bytes 7864324
  257.0 11.8 %copy-start.11 = (bf16[640,1280]{1,0:T(8,128)(2,1)S(1)}, bf16[640,1280]{1,0:T(8,128)(2,1)}, u32[]{:S(2)}) copy-start(bf16[640,1280]{1,0:T(8,128)(2,1)} %reshape.1474) | copy-start | bytes 4915204
  289.6 34.8 %collective-permute-start.5 = (bf16[1,640,64]{1,2,0:T(8,128)(2,1)S(1)}, bf16[1,640,64]{1,2,0:T(8,128)(2,1)S(1)}, u32[]{:S(2)}, u32[]{:S(2)}) collective-permute-start(bf16[1,640,64]{1,2,0:T(8,128)(2,1)S(1)} %get-tuple-element.103), channel_id=1, source_target_pairs={{0,4},{1,5},{2,6},{3,7},{8,12},{9,13},{10,14},{11,15},{16,20},{17,... | collective-permute-start | bytes 245768 | tf_op jit(solution)/shard_map/ppermute | solution.py:52
  292.7 30.8 %collective-permute-start.4 = (bf16[1,640,64]{1,2,0:T(8,128)(2,1)S(1)}, bf16[1,640,64]{1,2,0:T(8,128)(2,1)S(1)}, u32[]{:S(2)}, u32[]{:S(2)}) collective-permute-start(bf16[1,640,64]{1,2,0:T(8,128)(2,1)S(1)} %get-tuple-element.104), channel_id=1, source_target_pairs={{4,0},{5,1},{6,2},{7,3},{12,8},{13,9},{14,10},{15,11},{20,16},{21,... | collective-permute-start | bytes 245768 | tf_op jit(solution)/shard_map/ppermute | solution.py:53
  324.2 2.2 copy-start.10
  324.5 2.8 copy-start.2
  327.3 13.5 %copy-start.3 = (f32[1024,640]{1,0:T(8,128)S(1)}, f32[1024,640]{1,0:T(8,128)}, u32[]{:S(2)}) copy-start(f32[1024,640]{1,0:T(8,128)} %copy-done.1) | copy-start | bytes 7864324
  350.2 3.5 copy-start.13
  350.2 3.5 copy-start.15
  350.2 3.5 copy-start.17
  350.2 3.5 copy-start.19
  381.9 47.6 %copy-start.7 = (f32[4,204800]{1,0:T(4,128)S(1)}, f32[4,204800]{1,0:T(4,128)}, u32[]{:S(2)}) copy-start(f32[4,204800]{1,0:T(4,128)} %reshape.1491) | copy-start | bytes 9830404
  429.5 17.3 %copy-start.21 = (f32[4,320]{1,0:T(4,128)S(1)}, f32[4,320]{1,0:T(4,128)}, u32[]{:S(2)}) copy-start(f32[4,320]{1,0:T(4,128)} %convert_reduce_fusion.3) | copy-start | bytes 15364
  472.3 157.5 %reduce-scatter.8.cloned.1.call-start = ((), (), s32[]{:S(2)}) async-start(), calls=%async_computation.9 | async-start | bytes 9256960 | tf_op jit(solution)/shard_map/reduce_scatter | solution.py:221
  497.3 170.1 %copy-start.20 = (f32[4,320]{1,0:T(4,128)S(1)}, f32[4,320]{1,0:T(4,128)}, u32[]{:S(2)}) copy-start(f32[4,320]{1,0:T(4,128)} %get-tuple-element.114) | copy-start | bytes 15364
  497.3 170.2 %copy-start.9 = (f32[1024,640]{1,0:T(8,128)S(1)}, f32[1024,640]{1,0:T(8,128)}, u32[]{:S(2)}) copy-start(f32[1024,640]{1,0:T(8,128)} %copy-done.8) | copy-start | bytes 7864324
  497.3 170.1 %reduce-scatter.10.cloned.1.call-start = ((), (), s32[]{:S(2)}) async-start(), calls=%async_computation.11 | async-start | bytes 2314240
  629.8 166.6 %all-gather.7.cloned.1.call-start = ((), (), s32[]{:S(2)}) async-start(), calls=%async_computation.10 | async-start | bytes 4165632 | tf_op jit(solution)/shard_map/all_gather | solution.py:223
  710.0 43.0 %all-to-all-start.1 = ((bf16[4,2,163840]{2,1,0:T(2,128)(2,1)}), bf16[4,2,163840]{2,1,0:T(2,128)(2,1)}, u32[]{:S(2)}, u32[]{:S(2)}) async-start(bf16[4,2,163840]{2,1,0:T(2,128)(2,1)} %reshape.1509), calls=%async_computation.1 | async-start | bytes 5242880 | tf_op jit(solution)/shard_map/all_to_all | solution.py:77
  753.0 34.6 %all-to-all-start.3 = ((bf16[4,2,163840]{2,1,0:T(2,128)(2,1)}), bf16[4,2,163840]{2,1,0:T(2,128)(2,1)S(1)}, u32[]{:S(2)}, u32[]{:S(2)}) async-start(bf16[4,2,163840]{2,1,0:T(2,128)(2,1)} %reshape.1511), calls=%async_computation.3 | async-start | bytes 5242880 | tf_op jit(solution)/shard_map/all_to_all | solution.py:77
Sparse Core Ops, SparseCore 0:
  13.4 131.5 all-gather.4
  472.4 24.8 reduce-scatter.5
  499.7 130.0 reduce-scatter.7
  632.7 34.6 reduce-scatter.9
  668.8 42.8 all-gather.6
